TPU v7x, 32 devices: a whole 2x2x4 slice. The times are simulated.
32 devices in a mesh: rep: 2 (over x), ep: 4 (over y, core), grp: 4 (over z).
Axes of the slice: x: 2, y: 2, z: 4, core: 2. Of those that a mesh axis runs over, the one named last changes fastest.
Arguments:
- tokens: bfloat16 [4096, 4096], P(('rep', 'ep'), 'grp'), parts along dimension 0, may hold values from -6 to 6
- proj_in: bfloat16 [1024, 4096], P('ep', 'grp'), may hold values from -0.09375 to 0.09375
- proj_out: bfloat16 [1024, 4096], P('ep', 'grp'), may hold values from -0.1875 to 0.1875
- expert_up: bfloat16 [16, 1024, 2688], P(('ep', 'grp')), may hold values from -0.1875 to 0.1875
- expert_down: bfloat16 [16, 2688, 1024], P(('ep', 'grp')), may hold values from -0.125 to 0.125
- expert_ids: int32 [4096, 6], P(('rep', 'ep')), parts along dimension 0, may hold values from 0 to 15, as said below
- weight_codes: int32 [4096, 6], P(('rep', 'ep')), parts along dimension 0, may hold values from 1 to 64
Outputs:
- mixed: bfloat16 [4096, 4096], P(('rep', 'ep'), 'grp'), parts along dimension 0
There are 2 independent parts, one for each index of `rep`. A program takes and returns all parts, laid end to end along the dimension named above; an argument that names none is the same for every part. Nothing has to cross between parts.
Inputs may be any that keep to these rules, and one draw needn't show every extreme that they name: `expert_ids`: expert e belongs to group e % 4. Each token picks 6 distinct experts, two in each of 3 distinct groups. Within each aligned block of 128 tokens (the tokens of one device), every group is picked from by exactly 96 tokens, no expert is picked by more than 64 tokens, and in every block each group has an expert picked by exactly 64.
All inputs are finite; a program needn't handle non-finite values.
Results may differ from a plain program's by a relative error of at most 0.012.
Values may be sent and summed in bfloat16 or wider, within the bound.
A program may use at most 64 MiB of HBM per device.

v0:
```python
import jax
import jax.numpy as jnp
from jax import lax
from jax.sharding import PartitionSpec as P


def expert_block(arrived, expert_up, expert_down):
    width = arrived.shape[-1]
    flat_rows = arrived.reshape(-1, width)
    hidden = jnp.dot(flat_rows, expert_up[0], preferred_element_type=jnp.float32)
    hidden = jnp.square(jnp.maximum(hidden, 0.0)).astype(jnp.bfloat16)
    result = jnp.dot(hidden, expert_down[0], preferred_element_type=jnp.float32)
    return result.astype(jnp.bfloat16).reshape(arrived.shape)


def slot_positions(bucket, live, buckets):
    labels = jnp.arange(buckets, dtype=jnp.int32)
    onehot = jnp.logical_and(bucket[:, :, None] == labels, live[:, :, None]).astype(jnp.int32)
    per_row = jnp.sum(onehot, axis=1)
    before = jnp.cumsum(per_row, axis=0) - per_row
    return jnp.take_along_axis(before, bucket, axis=1)


def per_device(tokens, proj_in, proj_out, expert_up, expert_down, expert_ids, weight_codes):
    ep_count = lax.axis_size("ep")
    group_count = lax.axis_size("grp")
    experts = ep_count * group_count
    tok_block = tokens.shape[0]
    tok_dev = tok_block // group_count
    picks = expert_ids.shape[1]
    width = expert_up.shape[1]
    capacity = max(2, (4 * tok_dev * picks + 3 * experts - 1) // (3 * experts))
    in_rows, out_rows = (
        lax.all_gather(proj_in, "ep", axis=0, tiled=True),
        lax.all_gather(proj_out, "ep", axis=0, tiled=True),
    )
    latent = lax.psum_scatter(
        lax.dot_general(
            tokens, in_rows, (((1,), (1,)), ((), ())), preferred_element_type=jnp.float32
        ),
        "grp",
        scatter_dimension=0,
        tiled=True,
    ).astype(jnp.bfloat16)
    codes = weight_codes.astype(jnp.float32)
    route_weights = codes / jnp.sum(codes, axis=1, keepdims=True)
    group_index = lax.axis_index("grp")
    my_ids = lax.dynamic_slice_in_dim(expert_ids, group_index * tok_dev, tok_dev, 0)
    my_weights = lax.dynamic_slice_in_dim(route_weights, group_index * tok_dev, tok_dev, 0)
    position = slot_positions(my_ids, jnp.ones(my_ids.shape, jnp.bool_), experts)
    spread = jnp.broadcast_to(latent[:, None, :], (tok_dev, picks, width))
    outgoing = jnp.zeros((experts, capacity, width), jnp.bfloat16).at[my_ids, position].set(spread)
    computed = expert_block(
        lax.all_to_all(outgoing, ("ep", "grp"), split_axis=0, concat_axis=0, tiled=True),
        expert_up,
        expert_down,
    )
    returned = lax.all_to_all(computed, ("ep", "grp"), split_axis=0, concat_axis=0, tiled=True)
    picked = returned[my_ids, position]
    combined = jnp.sum(my_weights[:, :, None] * picked.astype(jnp.float32), axis=1)
    latent_out = combined.astype(jnp.bfloat16)
    mixed = jnp.dot(
        lax.all_gather(latent_out, "grp", axis=0, tiled=True),
        out_rows,
        preferred_element_type=jnp.float32,
    )
    return mixed.astype(jnp.bfloat16)


def solution(mesh):
    in_specs = (
        P(("rep", "ep"), "grp"),
        P("ep", "grp"),
        P("ep", "grp"),
        P(("ep", "grp"), None, None),
        P(("ep", "grp"), None, None),
        P(("rep", "ep"), None),
        P(("rep", "ep"), None),
    )
    out_specs = P(("rep", "ep"), "grp")
    return jax.shard_map(
        per_device, mesh=mesh, in_specs=in_specs, out_specs=out_specs, check_vma=False
    )
```

profile of v0, /device:TPU:0, one launch (start us, length us, event | category | flops | bytes accessed | tf_op | source)
XLA Modules:
  0.0 340.5 jit_solution(4923864919701778482)
XLA Ops:
  6.5 0.7 all-gather.4.cloned.1.call-update
  7.3 26.9 %all-gather.4.cloned.1.call-done = bf16[1024,1024]{1,0:T(8,128)(2,1)} async-done(((bf16[256,1024]{1,0:T(8,128)(2,1)}), bf16[1024,1024]{1,0:T(8,128)(2,1)}) %all-gather.4.cloned.1.call-update) | async-done | bytes 2097168 | tf_op jit(solution)/shard_map/all_gather | solution.py:34
  34.2 4.2 %fusion.16 = f32[512,1024]{1,0:T(8,128)} fusion(bf16[512,1024]{1,0:T(8,128)(2,1)S(1)} %copy-done, bf16[1024,1024]{1,0:T(8,128)(2,1)} %all-gather.4.cloned.1.call-done), kind=kOutput, calls=%fused_computation.29 | convolution fusion | flops 1073741824 | bytes 5242880 | tf_op jit(solution)/shard_map/dot_general | solution.py:38
  38.5 0.7 constant_dynamic-slice_fusion
  39.4 0.2 reduce_window_sum.11
  39.6 0.1 reshape.29
  39.7 5.1 %gather_fusion.1 = s32[768]{0:T(1024)S(1)} fusion(s32[128,16]{1,0:T(8,128)S(1)} %sub.3, s32[768]{0:T(1024)S(1)} %reshape.29), kind=kCustom, calls=%fused_computation.1 | custom fusion | bytes 12288 | tf_op jit(solution)/shard_map/jit(take_along_axis)/gather | solution.py:21
  45.2 37.0 %reduce-scatter.2.cloned.1.call-done = f32[128,1024]{1,0:T(8,128)} async-done(((f32[512,1024]{1,0:T(8,128)}), f32[128,1024]{1,0:T(8,128)}) %reduce-scatter.2.cloned.1.call-update) | async-done | bytes 524304 | tf_op jit(solution)/shard_map/reduce_scatter | solution.py:37
  82.3 1.1 convert_element_type.26
  83.4 0.3 broadcast_in_dim.13
  83.7 1.4 reshape.37
  85.1 0.3 broadcast_in_dim.10
  85.4 75.1 %scatter_fusion = bf16[16,64,1024]{2,1,0:T(8,128)(2,1)S(1)} fusion(bf16[16,64,1024]{2,1,0:T(8,128)(2,1)S(1)} %broadcast_in_dim.10, s32[768]{0:T(1024)S(1)} %reshape.35, bf16[768,1024]{1,0:T(8,128)(2,1)} %reshape.37), kind=kCustom, calls=%fused_computation.2 | custom fusion | bytes 4724736 | tf_op jit(solution)/shard_map/scatter | solution.py:52
  160.5 53.1 %all_to_all.10 = bf16[16,64,1024]{2,1,0:T(8,128)(2,1)} all-to-all(bf16[16,64,1024]{2,1,0:T(8,128)(2,1)S(1)} %scatter_fusion), channel_id=1, replica_groups=mesh['rep'=2,'ep'=4,'grp'=4] {'ep','grp'}, dimensions={0} | all-to-all | bytes 4194304 | tf_op jit(solution)/shard_map/all_to_all | solution.py:54
  213.7 18.2 %fusion.5 = bf16[1024,1024]{1,0:T(8,128)(2,1)} fusion(bf16[1,2688,1024]{2,1,0:T(8,128)(2,1)} %param.11, bf16[1024,1024]{1,0:T(8,128)(2,1)} %bitcast.43, bf16[1,1024,2688]{2,1,0:T(8,128)(2,1)} %param.10), kind=kOutput, calls=%fused_computation.9 | convolution fusion | flops 11283595264 | bytes 15204352 | tf_op jit(solution)/shard_map/dot_general | solution.py:12
  231.9 3.8 %all-to-all-start.1 = ((bf16[16,64,1024]{2,1,0:T(8,128)(2,1)}), bf16[16,64,1024]{2,1,0:T(8,128)(2,1)S(1)}, u32[]{:S(2)}, u32[]{:S(2)}) async-start(bf16[16,64,1024]{2,1,0:T(8,128)(2,1)} %bitcast.42), calls=%async_computation.2 | async-start | bytes 4194304 | tf_op jit(solution)/shard_map/all_to_all | solution.py:58
  235.8 0.7 all-gather.8.cloned.1.call-update
  236.5 0.3 all-gather.6.cloned.1.call-start
  237.1 47.9 %all-to-all-done.1 = bf16[16,64,1024]{2,1,0:T(8,128)(2,1)S(1)} async-done(((bf16[16,64,1024]{2,1,0:T(8,128)(2,1)}), bf16[16,64,1024]{2,1,0:T(8,128)(2,1)S(1)}, u32[]{:S(2)}, u32[]{:S(2)}) %all-to-all-start.1) | async-done | bytes 2097184 | tf_op jit(solution)/shard_map/all_to_all | solution.py:58
  285.0 9.8 %gather_fusion = bf16[768,1024]{1,0:T(8,128)(2,1)} fusion(bf16[16,64,1024]{2,1,0:T(8,128)(2,1)S(1)} %all-to-all-done.1, s32[768]{0:T(1024)S(1)} %reshape.23), kind=kCustom, calls=%fused_computation | custom fusion | bytes 3151872 | tf_op jit(solution)/shard_map/gather | solution.py:59
  294.8 3.9 %reshape.41 = f32[128,6,1024]{2,1,0:T(8,128)} reshape(bf16[768,1024]{1,0:T(8,128)(2,1)} %gather_fusion) | data formatting | bytes 4718592 | tf_op jit(solution)/shard_map/convert_element_type | solution.py:60
  298.7 4.3 %multiply_reduce_fusion = bf16[128,1024]{1,0:T(8,128)(2,1)} fusion(f32[128,6,1024]{2,1,0:T(8,128)} %reshape.41, f32[128,6]{1,0:T(8,128)S(1)} %copy.12), kind=kLoop, calls=%fused_computation.8 | loop fusion | flops 1441792 | bytes 3410944 | tf_op jit(solution)/shard_map/reduce_sum | solution.py:60
  303.0 26.8 %all-gather.6.cloned.1.call-done = bf16[512,1024]{1,0:T(8,128)(2,1)} async-done(((bf16[128,1024]{1,0:T(8,128)(2,1)}), bf16[512,1024]{1,0:T(8,128)(2,1)}) %all-gather.6.cloned.1.call-update) | async-done | bytes 1048592 | tf_op jit(solution)/shard_map/all_gather | solution.py:63
  329.9 4.1 %convolution_convert_fusion = bf16[512,1024]{1,0:T(8,128)(2,1)} fusion(bf16[512,1024]{1,0:T(8,128)(2,1)} %all-gather.6.cloned.1.call-done, bf16[1024,1024]{1,0:T(8,128)(2,1)} %all-gather.8.cloned.1.call-done), kind=kOutput, calls=%fused_computation.10 | convolution fusion | flops 1074266112 | bytes 4194304 | tf_op jit(solution)/shard_map/dot_general | solution.py:62
  (24 shorter events, 1.1 us)
Async XLA Ops:
  6.5 27.7 %copy-start = (bf16[512,1024]{1,0:T(8,128)(2,1)S(1)}, bf16[512,1024]{1,0:T(8,128)(2,1)}, u32[]{:S(2)}) copy-start(bf16[512,1024]{1,0:T(8,128)(2,1)} %param.7) | copy-start | bytes 3145732
  6.5 27.7 %all-gather.4.cloned.1.call-start = ((), (), s32[]{:S(2)}) async-start(), calls=%async_computation.3 | async-start | bytes 2621440 | tf_op jit(solution)/shard_map/all_gather | solution.py:34
  7.3 75.0 %reduce-scatter.2.cloned.1.call-start = ((), (), s32[]{:S(2)}) async-start(), calls=%async_computation.4 | async-start | bytes 2621440 | tf_op jit(solution)/shard_map/reduce_scatter | solution.py:37
  231.9 5.0 %copy-start.1 = (s32[512,6]{0,1:T(8,128)S(1)}, s32[512,6]{0,1:T(8,128)}, u32[]{:S(2)}) copy-start(s32[512,6]{0,1:T(8,128)} %param.13) | copy-start | bytes 36868
  231.9 53.2 %all-to-all-start.1 = ((bf16[16,64,1024]{2,1,0:T(8,128)(2,1)}), bf16[16,64,1024]{2,1,0:T(8,128)(2,1)S(1)}, u32[]{:S(2)}, u32[]{:S(2)}) async-start(bf16[16,64,1024]{2,1,0:T(8,128)(2,1)} %bitcast.42), calls=%async_computation.2 | async-start | bytes 4194304 | tf_op jit(solution)/shard_map/all_to_all | solution.py:58
  235.7 67.3 %all-gather.8.cloned.1.call-start = ((), (), s32[]{:S(2)}) async-start(), calls=%async_computation.6 | async-start | bytes 2621440 | tf_op jit(solution)/shard_map/all_gather | solution.py:35
  236.5 93.4 %all-gather.6.cloned.1.call-start = ((), (), s32[]{:S(2)}) async-start(), calls=%async_computation.5 | async-start | bytes 1310720 | tf_op jit(solution)/shard_map/all_gather | solution.py:63
Sparse Core Ops, SparseCore 0:
  8.9 25.2 all-gather.3
  38.6 43.6 reduce-scatter.1
  238.1 34.4 all-gather.7
  303.1 26.6 all-gather.5
where the time goes:
time: 344 us; the launch traced here: 341 us
  waiting for transfers between devices  140 us (41%)
  local copies, waits for them, and re-layouts  97.6 us (28%)
  blocking collectives  53.1 us (15%)
  matrix products  26.6 us (8%)
  between operations  13.3 us (4%)
  other arithmetic  5.68 us (2%)
  starting transfers between devices  4.19 us (1%)
    scatter x1, local copies, waits for them, and re-layouts, per_device(): jnp.zeros((experts, capacity, width), jnp.bfloat16).at[my_ids, position]  75.1 us
    all_to_all x1, blocking collectives, per_device(): lax.all_to_all(outgoing, ('ep', 'grp'), split_axis=0, concat_axis=0, tile...  53.1 us
    all_to_all x1, waiting for transfers between devices, per_device(): lax.all_to_all(computed, ('ep', 'grp'), split_axis=0, concat_axis=0, tile...  47.9 us
    reduce_scatter x1, waiting for transfers between devices, per_device(): lax.psum_scatter(lax.dot_general(tokens, in_rows, (((1,), (1,)), ((), ())...  37 us
    all_gather x1, waiting for transfers between devices, per_device(): lax.all_gather(proj_in, 'ep', axis=0, tiled=True)  26.9 us
    all_gather x1, waiting for transfers between devices, per_device(): lax.all_gather(latent_out, 'grp', axis=0, tiled=True)  26.8 us
    dot_general x1, matrix products, expert_block(): result = jnp.dot(hidden, expert_down[0], preferred_element_type=jnp.float32)  18.2 us
    gather x1, local copies, waits for them, and re-layouts, per_device(): picked = returned[my_ids, position]  9.77 us
  transfers between devices with their start and end apart: 5, of which 4 were waited for; matrix products, arithmetic and copies ran while one was open for 7% of the time, Pallas kernels for 0%

commit v1 on v0

--- a/solution.py
+++ b/solution.py
@@ -1,6 +1,10 @@
+import functools
+
 import jax
 import jax.numpy as jnp
 from jax import lax
+from jax.experimental import pallas as pl
+from jax.experimental.pallas import tpu as pltpu
 from jax.sharding import PartitionSpec as P
 
 
@@ -67,7 +71,359 @@
     return mixed.astype(jnp.bfloat16)
 
 
+MESH = pl.DeviceIdType.MESH
+BF = jnp.bfloat16
+F32 = jnp.float32
+
+
+def nt(a, b):
+    return lax.dot_general(a, b, (((1,), (1,)), ((), ())), preferred_element_type=F32)
+
+
+def nn(a, b):
+    return jnp.dot(a, b, preferred_element_type=F32)
+
+
+def fused_kernel(
+    groups, blocks, hits, cap,
+    tok, pin, pout, routing, up_hbm, down_hbm, out,
+    up, down, win, wout, meta, onehot_t, onehot, inv,
+    own, r1, l1, sr1, sl1, lat, xs, xin, hid, ys, mates, zsum, yret, sown, r2, l2, sr2, sl2,
+    hbm_sem, ag_s, ag_r, r1s, r1r, l1s, l1r, xss, xsr, ms, mr, yss, ysr, r2s, r2r, l2s, l2r,
+):
+    ep, z = lax.axis_index("ep"), lax.axis_index("grp")
+    chip = ep // 2
+    mate = chip * 2 + (1 - ep % 2)
+    ypart = (ep + 2) % 4
+    rows = tok.shape[0] // blocks
+    half = own.shape[2]
+    picks = routing.shape[0] // 2
+    far = jnp.maximum(z, groups - 1 - z)
+
+    def rcopy(src, dst, s, r, **dev):
+        return pltpu.make_async_remote_copy(
+            src_ref=src, dst_ref=dst, send_sem=s, recv_sem=r, device_id=dev, device_id_type=MESH
+        )
+
+    loads = [
+        pltpu.make_async_copy(up_hbm.at[0], up, hbm_sem.at[0]),
+        pltpu.make_async_copy(down_hbm.at[0], down, hbm_sem.at[1]),
+    ]
+
+    barrier = pltpu.get_barrier_semaphore()
+    for peer in (mate, ypart):
+        pl.semaphore_signal(barrier, inc=1, device_id={"ep": peer}, device_id_type=MESH)
+
+    @pl.when(z > 0)
+    def _():
+        pl.semaphore_signal(barrier, inc=1, device_id={"grp": z - 1}, device_id_type=MESH)
+
+    @pl.when(z < groups - 1)
+    def _():
+        pl.semaphore_signal(barrier, inc=1, device_id={"grp": z + 1}, device_id_type=MESH)
+
+    inner = jnp.logical_and(z > 0, z < groups - 1)
+    pl.semaphore_wait(barrier, jnp.where(inner, 4, 3))
+
+    def ag(kind, src, buf, at_own, at_y, mine_y, mine_mate, relay_to):
+        to_y = rcopy(src, buf.at[mine_y], ag_s.at[kind, 0], ag_r.at[kind, 0], ep=ypart)
+        to_mate = rcopy(src, buf.at[mine_mate], ag_s.at[kind, 1], ag_r.at[kind, 1], ep=mate)
+        relay = rcopy(buf.at[at_y], buf.at[relay_to], ag_s.at[kind, 2], ag_r.at[kind, 2], ep=mate)
+        return to_y, to_mate, relay
+
+    win_y, win_m, win_relay = ag(0, pin, win, ep, ypart, ep, ep, ypart)
+    wout_y, wout_m, wout_relay = ag(1, pout, wout, ep, ypart, ep, ep, ypart)
+    meta_y, meta_m, meta_relay = ag(2, meta.at[0], meta, 0, 1, 1, 2, 3)
+    win_y.start()
+    win_m.start()
+    for load in loads:
+        load.start()
+
+    ids = routing[0:picks, :]
+    codes = routing[picks : 2 * picks, :].astype(F32)
+    experts_here = lax.broadcasted_iota(jnp.int32, (8, ids.shape[1]), 0) * groups + z
+    table = jnp.zeros((8, ids.shape[1]), F32)
+    for p in range(picks):
+        table = table + jnp.where(ids[p : p + 1, :] == experts_here, codes[p : p + 1, :], 0.0)
+    inverse = 1.0 / jnp.sum(codes, axis=0, keepdims=True)
+    hit = jnp.where(jnp.sum(table, axis=0, keepdims=True) > 0.0, 1.0, 0.0)
+
+    def before(n):
+        i = lax.broadcasted_iota(jnp.int32, (n, n), 0)
+        j = lax.broadcasted_iota(jnp.int32, (n, n), 1)
+        return jnp.where(i < j, 1.0, 0.0).astype(BF)
+
+    def ranked(sel, count):
+        n = sel.shape[1]
+        rank = nn(jnp.broadcast_to(sel, (8, n)).astype(BF), before(n))[0:1, :]
+        slot = lax.broadcasted_iota(jnp.int32, (count, n), 0).astype(F32)
+        return jnp.where(jnp.logical_and(slot == rank, sel > 0.0), 1.0, 0.0)
+
+    for b in range(blocks):
+        at = slice(b * rows, (b + 1) * rows)
+        chosen = ranked(hit[:, at], hits)
+        onehot[b] = chosen.astype(BF)
+        onehot_t[b] = jnp.transpose(chosen).astype(BF)
+        meta[0, b] = nt(table[:, at].astype(BF), chosen.astype(BF))
+        inv[b] = jnp.transpose(jnp.broadcast_to(inverse[:, at], (rows, rows)))
+    meta_y.start()
+    meta_m.start()
+
+    win[ep] = pin[...]
+    wout[ep] = pout[...]
+    win_m.wait_recv()
+
+    def partial(h):
+        w = win[pl.ds(2 * jnp.where(h == 0, chip, 1 - chip), 2)].reshape(half, win.shape[2])
+        for b in range(blocks):
+            own[h * blocks + b] = nt(tok[b * rows : (b + 1) * rows, :], w)
+
+    def hop(k, recv, send, s, r, first, last, dest, mine):
+        @pl.when(jnp.logical_not(first))
+        def _():
+            rcopy(send.at[k], recv.at[k], s.at[k], r.at[k], grp=dest).wait_recv()
+
+        @pl.when(jnp.logical_not(last))
+        def _():
+            @pl.when(first)
+            def _():
+                send[k] = mine[k].astype(BF)
+
+            @pl.when(jnp.logical_not(first))
+            def _():
+                send[k] = (mine[k].astype(F32) + recv[k].astype(F32)).astype(BF)
+
+            rcopy(send.at[k], recv.at[k], s.at[k], r.at[k], grp=dest).start()
+
+    right = jnp.minimum(z + 1, groups - 1)
+    left = jnp.maximum(z - 1, 0)
+
+    def hops(t, n, bufs, mine):
+        rr, ll, ss, sl, rs_, rr_, ls_, lr_ = bufs
+        kr, kl = t - z, t - (groups - 1 - z)
+
+        @pl.when(jnp.logical_and(kr >= 0, kr < n))
+        def _():
+            hop(kr, rr, ss, rs_, rr_, z == 0, z == groups - 1, right, mine)
+
+        @pl.when(jnp.logical_and(kl >= 0, kl < n))
+        def _():
+            hop(kl, ll, sl, ls_, lr_, z == groups - 1, z == 0, left, mine)
+
+    def total(k, rr, ll, mine, finish):
+        @pl.when(z == 0)
+        def _():
+            finish(mine[k].astype(F32) + ll[k].astype(F32))
+
+        @pl.when(z == groups - 1)
+        def _():
+            finish(mine[k].astype(F32) + rr[k].astype(F32))
+
+        @pl.when(jnp.logical_and(z > 0, z < groups - 1))
+        def _():
+            finish(mine[k].astype(F32) + rr[k].astype(F32) + ll[k].astype(F32))
+
+    def x_copies(b):
+        return (
+            rcopy(xs.at[b, 0], xs.at[b, 1], xss.at[b, 0], xsr.at[b, 0], ep=ypart),
+            rcopy(xs.at[b, 0], xs.at[b, 2], xss.at[b, 1], xsr.at[b, 1], ep=mate),
+            rcopy(xs.at[b, 1], xs.at[b, 3], xss.at[b, 2], xsr.at[b, 2], ep=mate),
+        )
+
+    bufs1 = (r1, l1, sr1, sl1, r1s, r1r, l1s, l1r)
+    chunks = 2 * blocks
+
+    def step1(t, _):
+        hops(t, chunks, bufs1, own)
+        k = t - far
+
+        @pl.when(jnp.logical_and(k >= 0, k < chunks))
+        def _():
+            h = k // blocks
+            b = k % blocks
+            column = pl.multiple_of(jnp.where(h == 0, chip, 1 - chip) * half, half)
+
+            def finish(v):
+                lat[b, :, pl.ds(column, half)] = v.astype(BF)
+
+            total(k, r1, l1, own, finish)
+
+            @pl.when(h == 1)
+            def _():
+                xs[b, 0] = nn(onehot[b], lat[b]).astype(BF)
+                a, c, _ = x_copies(b)
+                a.start()
+                c.start()
+
+        return 0
+
+    partial(0)
+    lax.fori_loop(0, blocks, step1, 0)
+    win_y.wait_recv()
+    win_relay.start()
+    meta_y.wait_recv()
+    meta_relay.start()
+    wout_m.start()
+    wout_y.start()
+    win_relay.wait_recv()
+    partial(1)
+    lax.fori_loop(blocks, chunks + groups - 1, step1, 0)
+    for load in loads:
+        load.wait()
+    meta_m.wait_recv()
+    meta_relay.wait_recv()
+
+    def m_copy(b):
+        return rcopy(ys.at[b, pl.ds(2, 2)], mates.at[b], ms.at[b], mr.at[b], ep=mate)
+
+    def y_copy(b):
+        return rcopy(zsum.at[b, 1], yret.at[b], yss.at[b], ysr.at[b], ep=ypart)
+
+    bufs2 = (r2, l2, sr2, sl2, r2s, r2r, l2s, l2r)
+
+    def step2(u, _):
+        @pl.when(u < blocks)
+        def _():
+            b = u
+            a, c, relay = x_copies(b)
+            a.wait_recv()
+            relay.start()
+            c.wait_recv()
+            relay.wait_recv()
+            scaled = []
+            for s in range(4):
+                m = meta[s, b, pl.ds(ep, 1), :]
+                q = ranked(jnp.where(m > 0.0, 1.0, 0.0), cap)
+                xin[s * cap : (s + 1) * cap, :] = nn(q.astype(BF), xs[b, s]).astype(BF)
+                scaled.append(jnp.transpose(q * m).astype(BF))
+            h = jnp.maximum(nn(xin[...], up[...]), 0.0)
+            hid[...] = (h * h).astype(BF)
+            o = nn(hid[...], down[...]).astype(BF)
+            for s in range(4):
+                ys[b, s] = nn(scaled[s], o[s * cap : (s + 1) * cap, :]).astype(BF)
+            m_copy(b).start()
+
+        @pl.when(jnp.logical_and(u >= 1, u < blocks + 1))
+        def _():
+            b = u - 1
+            m_copy(b).wait_recv()
+            zsum[b] = (ys[b, 0:2].astype(F32) + mates[b].astype(F32)).astype(BF)
+            y_copy(b).start()
+
+        @pl.when(u == 1)
+        def _():
+            wout_y.wait_recv()
+            wout_relay.start()
+
+        @pl.when(jnp.logical_and(u >= 2, u < blocks + 2))
+        def _():
+            b = u - 2
+            y_copy(b).wait_recv()
+            v = (zsum[b, 0].astype(F32) + yret[b].astype(F32)).astype(BF)
+            sown[b] = nn(onehot_t[b], v).astype(BF)
+
+        @pl.when(u == 3)
+        def _():
+            wout_m.wait_recv()
+            wout_relay.wait_recv()
+
+        t = u - 2
+        hops(t, blocks, bufs2, sown)
+        k = t - far
+
+        @pl.when(jnp.logical_and(k >= 0, k < blocks))
+        def _():
+            def finish(v):
+                w = jnp.concatenate([inv[k]] * (v.shape[1] // rows), axis=1)
+                y = (v * w).astype(BF)
+                full = wout[...].reshape(v.shape[1], wout.shape[2])
+                out[pl.ds(pl.multiple_of(k * rows, rows), rows), :] = nn(y, full).astype(BF)
+
+            total(k, r2, l2, sown, finish)
+
+        return 0
+
+    lax.fori_loop(0, blocks + 2 + groups - 1, step2, 0)
+
+    for copy in (win_y, win_m, win_relay, wout_y, wout_m, wout_relay, meta_y, meta_m, meta_relay):
+        copy.wait_send()
+
+    def drain(n, bufs):
+        rr, ll, ss, sl, rs_, rr_, ls_, lr_ = bufs
+
+        @pl.when(z < groups - 1)
+        def _():
+            for k in range(n):
+                rcopy(ss.at[k], rr.at[k], rs_.at[k], rr_.at[k], grp=right).wait_send()
+
+        @pl.when(z > 0)
+        def _():
+            for k in range(n):
+                rcopy(sl.at[k], ll.at[k], ls_.at[k], lr_.at[k], grp=left).wait_send()
+
+    drain(chunks, bufs1)
+    drain(blocks, bufs2)
+    for b in range(blocks):
+        for copy in x_copies(b):
+            copy.wait_send()
+        m_copy(b).wait_send()
+        y_copy(b).wait_send()
+
+
+def fused_device(sizes, tokens, proj_in, proj_out, expert_up, expert_down, expert_ids, weight_codes):
+    groups = sizes["grp"]
+    blocks = groups
+    rows = tokens.shape[0] // blocks
+    picks = expert_ids.shape[1]
+    experts = sizes["ep"] * groups
+    hits = rows * (picks // 2) // groups
+    cap = max(2, (4 * rows * picks + 3 * experts - 1) // (3 * experts))
+    latent, features = proj_in.shape[0] * sizes["ep"], proj_in.shape[1]
+    hidden = expert_up.shape[2]
+    half = latent // 2
+    routing = jnp.concatenate([expert_ids.T, weight_codes.T], axis=0)
+    chunks = 2 * blocks
+    vm = pltpu.VMEM
+    dma = pltpu.SemaphoreType.DMA
+    scratch = [
+        vm((latent, hidden), BF), vm((hidden, latent), BF),
+        vm((4, *proj_in.shape), BF), vm((4, *proj_out.shape), BF),
+        vm((4, blocks, 8, hits), F32), vm((blocks, rows, hits), BF), vm((blocks, hits, rows), BF),
+        vm((blocks, rows, rows), F32),
+        vm((chunks, rows, half), F32),
+        *[vm((chunks, rows, half), BF)] * 4,
+        vm((blocks, rows, latent), BF),
+        vm((blocks, 4, hits, latent), BF),
+        vm((4 * cap, latent), BF), vm((4 * cap, hidden), BF),
+        vm((blocks, 4, hits, latent), BF),
+        vm((blocks, 2, hits, latent), BF), vm((blocks, 2, hits, latent), BF),
+        vm((blocks, hits, latent), BF),
+        vm((blocks, rows, latent), BF),
+        *[vm((blocks, rows, latent), BF)] * 4,
+        dma((2,)), dma((3, 3)), dma((3, 3)),
+        *[dma((chunks,))] * 4,
+        dma((blocks, 3)), dma((blocks, 3)),
+        *[dma((blocks,))] * 8,
+    ]
+    vmem = pl.BlockSpec(memory_space=pltpu.VMEM)
+    hbm = pl.BlockSpec(memory_space=pl.ANY)
+    return pl.pallas_call(
+        functools.partial(fused_kernel, groups, blocks, hits, cap),
+        out_shape=jax.ShapeDtypeStruct((tokens.shape[0], features), BF),
+        in_specs=[vmem, vmem, vmem, vmem, hbm, hbm],
+        out_specs=vmem,
+        scratch_shapes=scratch,
+        compiler_params=pltpu.CompilerParams(
+            collective_id=0, has_side_effects=True, vmem_limit_bytes=60 << 20
+        ),
+    )(tokens, proj_in, proj_out, routing, expert_up, expert_down)
+
+
 def solution(mesh):
+    sizes = dict(mesh.shape)
+    body = per_device
+    if sizes["ep"] == 4 and sizes["grp"] <= 4:
+        body = functools.partial(fused_device, sizes)
     in_specs = (
         P(("rep", "ep"), "grp"),
         P("ep", "grp"),
@@ -79,5 +435,5 @@
     )
     out_specs = P(("rep", "ep"), "grp")
     return jax.shard_map(
-        per_device, mesh=mesh, in_specs=in_specs, out_specs=out_specs, check_vma=False
+        body, mesh=mesh, in_specs=in_specs, out_specs=out_specs, check_vma=False
     )

time: 344 us -> 121 us (0.35)
  waiting for transfers between devices: 140 us -> 0 us
  Pallas kernels: 0 us -> 117 us
  local copies, waits for them, and re-layouts: 97.6 us -> 2.26 us
  blocking collectives: 53.1 us -> 0 us
  matrix products: 26.6 us -> 0 us
  between operations: 13.3 us -> 0.01 us
  other arithmetic: 5.68 us -> 1.36 us
  starting transfers between devices: 4.19 us -> 0 us
    pallas_call x0 -> x1, Pallas kernels: none -> 117 us  [fused_device(): pl.pallas_call(functools.partial(fused_kernel, groups, blocks, hits, cap)...]
    scatter x1 -> x0, local copies, waits for them, and re-layouts: 75.1 us -> none  [per_device(): jnp.zeros((experts, capacity, width), jnp.bfloat16).at[my_ids, position]]
    all_gather x3 -> x0, waiting for transfers between devices: 53.8 us -> none  [the longest x1 26.9 us: per_device(): lax.all_gather(proj_in, 'ep', axis=0, tiled=True)]
    all_to_all x1 -> x0, blocking collectives: 53.1 us -> none  [per_device(): lax.all_to_all(outgoing, ('ep', 'grp'), split_axis=0, concat_axis=0, tile...]
    all_to_all x1 -> x0, waiting for transfers between devices: 47.9 us -> none  [per_device(): lax.all_to_all(computed, ('ep', 'grp'), split_axis=0, concat_axis=0, tile...]
    reduce_scatter x1 -> x0, waiting for transfers between devices: 37 us -> none  [per_device(): lax.psum_scatter(lax.dot_general(tokens, in_rows, (((1,), (1,)), ((), ())...]
    dot_general x3 -> x0, matrix products: 26.6 us -> none  [the longest x1 18.2 us: expert_block(): result = jnp.dot(hidden, expert_down[0], preferred_element_type=jnp.float32)]
    gather x4 -> x0, local copies, waits for them, and re-layouts: 15.2 us -> none  [the longest x1 9.77 us: per_device(): picked = returned[my_ids, position]]
  transfers between devices with their start and end apart: 5 -> 0, of which waited for: 4 -> 0; matrix products, arithmetic and copies ran while one was open for 7% -> 0% of each run, Pallas kernels for 0% -> 0%
where the time goes in v1:
time: 121 us; the launch traced here: 120 us
  Pallas kernels  117 us (97%)
  local copies, waits for them, and re-layouts  2.26 us (2%)
  other arithmetic  1.36 us (1%)
    pallas_call x1, Pallas kernels, fused_device(): pl.pallas_call(functools.partial(fused_kernel, groups, blocks, hits, cap)...  117 us

profile of v1, /device:TPU:0, one launch (start us, length us, event | category | flops | bytes accessed | tf_op | source)
XLA Modules:
  0.0 120.3 jit_solution(12767269831147531446)
XLA Ops:
  0.0 1.4 %pad_add_fusion.routing = s32[12,512]{1,0:T(8,128)} fusion(s32[6,512]{1,0:T(8,128)} %bitcast.2, s32[6,512]{1,0:T(8,128)} %bitcast.3), kind=kLoop, calls=%fused_computation | loop fusion | flops 6144 | bytes 49152 | tf_op jit(solution)/shard_map/concatenate | solution.py:384
  1.4 116.7 %shard_map.73 = bf16[512,1024]{1,0:T(8,128)(2,1)} custom-call(bf16[512,1024]{1,0:T(8,128)(2,1)} %tok.1, bf16[256,1024]{1,0:T(8,128)(2,1)} %pin.1, bf16[256,1024]{1,0:T(8,128)(2,1)} %pout.1, s32[12,512]{1,0:T(8,128)} %pad_add_fusion.routing, bf16[1,1024,2688]{2,1,0:T(8,128)(2,1)} %up_hbm.1, bf16[1,2688,1024]{2,1,0:T(8,128)(2,1)} %down_hbm.1), custom_call_target="tpu_custom_call" | custom-call | tf_op jit(solution)/shard_map/pallas_call | solution.py:410
  118.1 2.3 %copy.9 = bf16[512,1024]{1,0:T(8,128)(2,1)} copy(bf16[512,1024]{1,0:T(8,128)(2,1)} %shard_map.73) | data formatting | bytes 2097152

commit v2 on v1

--- a/solution.py
+++ b/solution.py
@@ -91,7 +91,7 @@
     own, r1, l1, sr1, sl1, lat, xs, xin, hid, ys, mates, zsum, yret, sown, r2, l2, sr2, sl2,
     hbm_sem, ag_s, ag_r, r1s, r1r, l1s, l1r, xss, xsr, ms, mr, yss, ysr, r2s, r2r, l2s, l2r,
 ):
-    ep, z = lax.axis_index("ep"), lax.axis_index("grp")
+    ep, z, part = lax.axis_index("ep"), lax.axis_index("grp"), lax.axis_index("rep")
     chip = ep // 2
     mate = chip * 2 + (1 - ep % 2)
     ypart = (ep + 2) % 4
@@ -113,6 +113,7 @@
     barrier = pltpu.get_barrier_semaphore()
     for peer in (mate, ypart):
         pl.semaphore_signal(barrier, inc=1, device_id={"ep": peer}, device_id_type=MESH)
+    pl.semaphore_signal(barrier, inc=1, device_id={"rep": 1 - part}, device_id_type=MESH)
 
     @pl.when(z > 0)
     def _():
@@ -123,17 +124,30 @@
         pl.semaphore_signal(barrier, inc=1, device_id={"grp": z + 1}, device_id_type=MESH)
 
     inner = jnp.logical_and(z > 0, z < groups - 1)
-    pl.semaphore_wait(barrier, jnp.where(inner, 4, 3))
-
-    def ag(kind, src, buf, at_own, at_y, mine_y, mine_mate, relay_to):
-        to_y = rcopy(src, buf.at[mine_y], ag_s.at[kind, 0], ag_r.at[kind, 0], ep=ypart)
-        to_mate = rcopy(src, buf.at[mine_mate], ag_s.at[kind, 1], ag_r.at[kind, 1], ep=mate)
-        relay = rcopy(buf.at[at_y], buf.at[relay_to], ag_s.at[kind, 2], ag_r.at[kind, 2], ep=mate)
-        return to_y, to_mate, relay
-
-    win_y, win_m, win_relay = ag(0, pin, win, ep, ypart, ep, ep, ypart)
-    wout_y, wout_m, wout_relay = ag(1, pout, wout, ep, ypart, ep, ep, ypart)
-    meta_y, meta_m, meta_relay = ag(2, meta.at[0], meta, 0, 1, 1, 2, 3)
+    pl.semaphore_wait(barrier, jnp.where(inner, 5, 4))
+
+    share = pin.shape[0] // 2
+    my_share = pl.ds(pl.multiple_of(part * share, share), share)
+    peer_share = pl.ds(pl.multiple_of((1 - part) * share, share), share)
+
+    def ag(kind, src, buf):
+        def one(i, a, b, **dev):
+            return rcopy(a, b, ag_s.at[kind, i], ag_r.at[kind, i], **dev)
+
+        first, second = buf.at[ypart, my_share], buf.at[ypart, peer_share]
+        return (
+            one(0, src.at[my_share], buf.at[ep, my_share], ep=ypart),
+            one(1, src, buf.at[ep], ep=mate),
+            one(2, first, first, ep=mate),
+            one(3, first, first, rep=1 - part),
+            one(4, second, second, ep=mate),
+        )
+
+    win_y, win_m, win_relay, win_x, win_relay2 = ag(0, pin, win)
+    wout_y, wout_m, wout_relay, wout_x, wout_relay2 = ag(1, pout, wout)
+    meta_y = rcopy(meta.at[0], meta.at[1], ag_s.at[2, 0], ag_r.at[2, 0], ep=ypart)
+    meta_m = rcopy(meta.at[0], meta.at[2], ag_s.at[2, 1], ag_r.at[2, 1], ep=mate)
+    meta_relay = rcopy(meta.at[1], meta.at[3], ag_s.at[2, 2], ag_r.at[2, 2], ep=mate)
     win_y.start()
     win_m.start()
     for load in loads:
@@ -176,7 +190,7 @@
     def partial(h):
         w = win[pl.ds(2 * jnp.where(h == 0, chip, 1 - chip), 2)].reshape(half, win.shape[2])
         for b in range(blocks):
-            own[h * blocks + b] = nt(tok[b * rows : (b + 1) * rows, :], w)
+            own[2 * (b // 2) * 2 + 2 * h + b % 2] = nt(tok[b * rows : (b + 1) * rows, :], w)
 
     def hop(k, recv, send, s, r, first, last, dest, mine):
         @pl.when(jnp.logical_not(first))
@@ -239,8 +253,8 @@
 
         @pl.when(jnp.logical_and(k >= 0, k < chunks))
         def _():
-            h = k // blocks
-            b = k % blocks
+            h = k % 4 // 2
+            b = k // 4 * 2 + k % 2
             column = pl.multiple_of(jnp.where(h == 0, chip, 1 - chip) * half, half)
 
             def finish(v):
@@ -257,95 +271,122 @@
 
         return 0
 
+    def m_copy(b):
+        return rcopy(ys.at[b, pl.ds(2, 2)], mates.at[b], ms.at[b], mr.at[b], ep=mate)
+
+    def y_copy(b):
+        return rcopy(zsum.at[b, 1], yret.at[b], yss.at[b], ysr.at[b], ep=ypart)
+
+    bufs2 = (r2, l2, sr2, sl2, r2s, r2r, l2s, l2r)
+
+    def relay_x(b):
+        a, _, relay = x_copies(b)
+        a.wait_recv()
+        relay.start()
+
+    def expert(b):
+        _, c, relay = x_copies(b)
+        c.wait_recv()
+        relay.wait_recv()
+        scaled = []
+        for s in range(4):
+            m = meta[s, b, pl.ds(ep, 1), :]
+            q = ranked(jnp.where(m > 0.0, 1.0, 0.0), cap)
+            xin[s * cap : (s + 1) * cap, :] = nn(q.astype(BF), xs[b, s]).astype(BF)
+            scaled.append(jnp.transpose(q * m).astype(BF))
+        h = jnp.maximum(nn(xin[...], up[...]), 0.0)
+        hid[...] = (h * h).astype(BF)
+        o = nn(hid[...], down[...]).astype(BF)
+        for s in (2, 3, 0, 1):
+            ys[b, s] = nn(scaled[s], o[s * cap : (s + 1) * cap, :]).astype(BF)
+            if s == 3:
+                m_copy(b).start()
+
+    def pair(b):
+        m_copy(b).wait_recv()
+        zsum[b, 1] = (ys[b, 1].astype(F32) + mates[b, 1].astype(F32)).astype(BF)
+        y_copy(b).start()
+        zsum[b, 0] = (ys[b, 0].astype(F32) + mates[b, 0].astype(F32)).astype(BF)
+
+    def home(b):
+        y_copy(b).wait_recv()
+        v = (zsum[b, 0].astype(F32) + yret[b].astype(F32)).astype(BF)
+        for c in range(2):
+            sown[2 * b + c] = nn(onehot_t[b], v[:, c * half : (c + 1) * half]).astype(BF)
+
+    def step2(t, _):
+        hops(t, chunks, bufs2, sown)
+        k = t - far
+
+        @pl.when(jnp.logical_and(k >= 0, k < chunks))
+        def _():
+            b = k // 2
+            column = pl.multiple_of(k % 2 * half, half)
+
+            def finish(v):
+                w = jnp.concatenate([inv[b]] * (half // rows), axis=1)
+                lat[b, :, pl.ds(column, half)] = (v * w).astype(BF)
+
+            total(k, r2, l2, sown, finish)
+
+            @pl.when(k % 2 == 1)
+            def _():
+                full = wout[...].reshape(2 * half, wout.shape[2])
+                out[pl.ds(pl.multiple_of(b * rows, rows), rows), :] = nn(lat[b], full).astype(BF)
+
+        return 0
+
     partial(0)
-    lax.fori_loop(0, blocks, step1, 0)
+    lax.fori_loop(0, 2, step1, 0)
     win_y.wait_recv()
     win_relay.start()
+    win_x.start()
     meta_y.wait_recv()
     meta_relay.start()
     wout_m.start()
     wout_y.start()
+    win_x.wait_recv()
+    win_relay2.start()
     win_relay.wait_recv()
+    win_relay2.wait_recv()
     partial(1)
-    lax.fori_loop(blocks, chunks + groups - 1, step1, 0)
+    steps = chunks + groups - 1
+    lax.fori_loop(2, 7, step1, 0)
+    relay_x(0)
+    lax.fori_loop(7, 8, step1, 0)
     for load in loads:
         load.wait()
     meta_m.wait_recv()
     meta_relay.wait_recv()
-
-    def m_copy(b):
-        return rcopy(ys.at[b, pl.ds(2, 2)], mates.at[b], ms.at[b], mr.at[b], ep=mate)
-
-    def y_copy(b):
-        return rcopy(zsum.at[b, 1], yret.at[b], yss.at[b], ysr.at[b], ep=ypart)
-
-    bufs2 = (r2, l2, sr2, sl2, r2s, r2r, l2s, l2r)
-
-    def step2(u, _):
-        @pl.when(u < blocks)
-        def _():
-            b = u
-            a, c, relay = x_copies(b)
-            a.wait_recv()
-            relay.start()
-            c.wait_recv()
-            relay.wait_recv()
-            scaled = []
-            for s in range(4):
-                m = meta[s, b, pl.ds(ep, 1), :]
-                q = ranked(jnp.where(m > 0.0, 1.0, 0.0), cap)
-                xin[s * cap : (s + 1) * cap, :] = nn(q.astype(BF), xs[b, s]).astype(BF)
-                scaled.append(jnp.transpose(q * m).astype(BF))
-            h = jnp.maximum(nn(xin[...], up[...]), 0.0)
-            hid[...] = (h * h).astype(BF)
-            o = nn(hid[...], down[...]).astype(BF)
-            for s in range(4):
-                ys[b, s] = nn(scaled[s], o[s * cap : (s + 1) * cap, :]).astype(BF)
-            m_copy(b).start()
-
-        @pl.when(jnp.logical_and(u >= 1, u < blocks + 1))
-        def _():
-            b = u - 1
-            m_copy(b).wait_recv()
-            zsum[b] = (ys[b, 0:2].astype(F32) + mates[b].astype(F32)).astype(BF)
-            y_copy(b).start()
-
-        @pl.when(u == 1)
-        def _():
-            wout_y.wait_recv()
-            wout_relay.start()
-
-        @pl.when(jnp.logical_and(u >= 2, u < blocks + 2))
-        def _():
-            b = u - 2
-            y_copy(b).wait_recv()
-            v = (zsum[b, 0].astype(F32) + yret[b].astype(F32)).astype(BF)
-            sown[b] = nn(onehot_t[b], v).astype(BF)
-
-        @pl.when(u == 3)
-        def _():
+    expert(0)
+    relay_x(1)
+    pair(0)
+    lax.fori_loop(8, steps, step1, 0)
+    wout_y.wait_recv()
+    wout_relay.start()
+    wout_x.start()
+    for b in range(1, blocks):
+        expert(b)
+        if b == 1:
+            wout_x.wait_recv()
+            wout_relay2.start()
+        if b + 1 < blocks:
+            relay_x(b + 1)
+        home(b - 1)
+        if b == 2:
             wout_m.wait_recv()
             wout_relay.wait_recv()
-
-        t = u - 2
-        hops(t, blocks, bufs2, sown)
-        k = t - far
-
-        @pl.when(jnp.logical_and(k >= 0, k < blocks))
-        def _():
-            def finish(v):
-                w = jnp.concatenate([inv[k]] * (v.shape[1] // rows), axis=1)
-                y = (v * w).astype(BF)
-                full = wout[...].reshape(v.shape[1], wout.shape[2])
-                out[pl.ds(pl.multiple_of(k * rows, rows), rows), :] = nn(y, full).astype(BF)
-
-            total(k, r2, l2, sown, finish)
-
-        return 0
-
-    lax.fori_loop(0, blocks + 2 + groups - 1, step2, 0)
-
-    for copy in (win_y, win_m, win_relay, wout_y, wout_m, wout_relay, meta_y, meta_m, meta_relay):
+            wout_relay2.wait_recv()
+        lax.fori_loop(2 * (b - 1), 2 * b, step2, 0)
+        pair(b)
+    home(blocks - 1)
+    lax.fori_loop(2 * (blocks - 1), steps, step2, 0)
+
+    for copy in (
+        *(win_y, win_m, win_relay, win_x, win_relay2),
+        *(wout_y, wout_m, wout_relay, wout_x, wout_relay2),
+        *(meta_y, meta_m, meta_relay),
+    ):
         copy.wait_send()
 
     def drain(n, bufs):
@@ -362,7 +403,7 @@
                 rcopy(sl.at[k], ll.at[k], ls_.at[k], lr_.at[k], grp=left).wait_send()
 
     drain(chunks, bufs1)
-    drain(blocks, bufs2)
+    drain(chunks, bufs2)
     for b in range(blocks):
         for copy in x_copies(b):
             copy.wait_send()
@@ -398,12 +439,12 @@
         vm((blocks, 4, hits, latent), BF),
         vm((blocks, 2, hits, latent), BF), vm((blocks, 2, hits, latent), BF),
         vm((blocks, hits, latent), BF),
-        vm((blocks, rows, latent), BF),
-        *[vm((blocks, rows, latent), BF)] * 4,
-        dma((2,)), dma((3, 3)), dma((3, 3)),
+        *[vm((chunks, rows, half), BF)] * 5,
+        dma((2,)), dma((3, 5)), dma((3, 5)),
         *[dma((chunks,))] * 4,
         dma((blocks, 3)), dma((blocks, 3)),
-        *[dma((blocks,))] * 8,
+        *[dma((blocks,))] * 4,
+        *[dma((chunks,))] * 4,
     ]
     vmem = pl.BlockSpec(memory_space=pltpu.VMEM)
     hbm = pl.BlockSpec(memory_space=pl.ANY)
@@ -422,7 +463,7 @@
 def solution(mesh):
     sizes = dict(mesh.shape)
     body = per_device
-    if sizes["ep"] == 4 and sizes["grp"] <= 4:
+    if sizes["rep"] == 2 and sizes["ep"] == 4 and sizes["grp"] == 4:
         body = functools.partial(fused_device, sizes)
     in_specs = (
         P(("rep", "ep"), "grp"),

time: 121 us -> 123 us (1.017)
  Pallas kernels: 117 us -> 119 us
    pallas_call x1, Pallas kernels: 117 us -> 119 us  [fused_device(): pl.pallas_call(functools.partial(fused_kernel, groups, blocks, hits, cap)...]
where the time goes in v2:
time: 123 us
  Pallas kernels  119 us (97%)
  local copies, waits for them, and re-layouts  2.26 us (2%)
  other arithmetic  1.36 us (1%)
    pallas_call x1, Pallas kernels, fused_device(): pl.pallas_call(functools.partial(fused_kernel, groups, blocks, hits, cap)...  119 us

profile of v2, /device:TPU:0, one launch (start us, length us, event | category | flops | bytes accessed | tf_op | source)
XLA Modules:
  0.0 122.9 jit_solution(8126790470984401150)
XLA Ops:
  0.0 1.4 %pad_add_fusion.routing = s32[12,512]{1,0:T(8,128)} fusion(s32[6,512]{1,0:T(8,128)} %bitcast.2, s32[6,512]{1,0:T(8,128)} %bitcast.3), kind=kLoop, calls=%fused_computation | loop fusion | flops 6144 | bytes 49152 | tf_op jit(solution)/shard_map/concatenate | solution.py:425
  1.4 119.2 %shard_map.73 = bf16[512,1024]{1,0:T(8,128)(2,1)} custom-call(bf16[512,1024]{1,0:T(8,128)(2,1)} %tok.1, bf16[256,1024]{1,0:T(8,128)(2,1)} %pin.1, bf16[256,1024]{1,0:T(8,128)(2,1)} %pout.1, s32[12,512]{1,0:T(8,128)} %pad_add_fusion.routing, bf16[1,1024,2688]{2,1,0:T(8,128)(2,1)} %up_hbm.1, bf16[1,2688,1024]{2,1,0:T(8,128)(2,1)} %down_hbm.1), custom_call_target="tpu_custom_call" | custom-call | tf_op jit(solution)/shard_map/pallas_call | solution.py:451
  120.6 2.3 %copy.9 = bf16[512,1024]{1,0:T(8,128)(2,1)} copy(bf16[512,1024]{1,0:T(8,128)(2,1)} %shard_map.73) | data formatting | bytes 2097152
